TPU v7x, 256 devices: a whole 4x4x8 slice. The times are simulated.
256 devices in a mesh: node: 32 (over z, x), feat: 8 (over y, core).
Axes of the slice: x: 4, y: 4, z: 8, core: 2. Of those that a mesh axis runs over, the one named last changes fastest.
Arguments:
- out_grad: bfloat16 [256, 262144], P('feat', 'node'), may hold values from -6 to 6
- pre_act: bfloat16 [256, 262144], P('feat', 'node'), may hold values from -6 to 6
- in_act: bfloat16 [256, 262144], P(None, ('node', 'feat')), may hold values from -6 to 6
- weight: bfloat16 [256, 256], replicated, may hold values from -0.375 to 0.375
- tiles: bfloat16 [2048, 24, 128, 128], P('node'), may hold values from -0.4375 to 0.4375
- indices: int32 [2048, 24], P('node'), may hold values from 0 to 2047, as said below
- counts: int32 [2048], P('node'), may hold values from 1 to 24, as said below
Outputs:
- in_grad: bfloat16 [256, 262144], P(None, ('node', 'feat'))
- weight_grad: float32 [256, 256], replicated
Inputs may be any that keep to these rules, and one draw needn't show every extreme that they name: `indices`: the 24 column blocks named by one row block are distinct; slots at or after the row block's count are ignored. Each node device has a cap between 2 and 24, and its row blocks' counts are at most that cap, except for one row block in the whole graph whose count is 24.
All inputs are finite; a program needn't handle non-finite values.
Results may differ from a plain program's by a relative error of at most 0.012.
Values may be sent and summed in bfloat16 or wider, within the bound.
No kernel may reach another device: no remote copies, remote signals or barrier semaphores. Data moves between devices by JAX's collectives and lax.ppermute only.
A program may use at most 192 MiB of HBM per device.

v0:
```python
import jax
import jax.numpy as jnp
from jax import lax
from jax.sharding import PartitionSpec as P


def sent_to_all(shard, axis):
    size = lax.axis_size(axis)
    return lax.all_to_all(
        jnp.broadcast_to(shard[None], (size, *shard.shape)), axis, 0, 0, tiled=True
    )


def over_copies(shard, axis):
    everything = sent_to_all(shard, axis)
    return jnp.sum(everything.astype(jnp.float32), axis=0)


def laid_out(tiles, dim):
    lengths = list(tiles.shape[1:])
    lengths[dim] *= tiles.shape[0]
    return jnp.moveaxis(tiles, 0, dim).reshape(lengths)


def collect(shard, axis, dim):
    return laid_out(sent_to_all(shard, axis), dim)


def per_device(out_grad, pre_act, in_act, weight, tiles, indices, counts):
    grad_pre = jnp.where(pre_act > 0, out_grad, jnp.zeros_like(out_grad))
    whole = lax.all_gather(grad_pre, "node", axis=1, tiled=True)
    feat_rows = whole.shape[0]
    block_size = tiles.shape[2]
    slot_count = tiles.shape[1]
    local_rows = grad_pre.shape[1]
    blocks = whole.reshape(feat_rows, whole.shape[1] // block_size, block_size)
    picked = jnp.take(blocks, indices, axis=1)
    slots = jnp.arange(slot_count, dtype=jnp.int32)
    live = (slots[None, :] < counts[:, None]).astype(jnp.bfloat16)
    picked = picked * live[None, :, :, None]
    summed = jnp.einsum("frkc,rkic->fri", picked, tiles, preferred_element_type=jnp.float32)
    aggregated = summed.reshape(feat_rows, local_rows).astype(jnp.bfloat16)
    scale = float(whole.shape[1]) ** (-0.5)
    node_rows = lax.all_to_all(aggregated, "feat", split_axis=1, concat_axis=0, tiled=True)
    in_grad = jnp.dot(weight, node_rows, preferred_element_type=jnp.float32).astype(jnp.bfloat16)
    group_acts = lax.all_gather(in_act, "feat", axis=1, tiled=True)
    column_part = (
        lax.dot_general(
            group_acts, aggregated, (((1,), (1,)), ((), ())), preferred_element_type=jnp.float32
        )
        * scale
    )
    column_part = over_copies(column_part.astype(jnp.bfloat16), "node").astype(jnp.float32)
    weight_grad = collect(column_part.astype(jnp.bfloat16), "feat", 1).astype(column_part.dtype)
    return (in_grad, weight_grad)


def solution(mesh):
    in_specs = (
        P("feat", "node"),
        P("feat", "node"),
        P(None, ("node", "feat")),
        P(),
        P("node", None, None, None),
        P("node", None),
        P("node"),
    )
    out_specs = (P(None, ("node", "feat")), P())
    return jax.shard_map(
        per_device, mesh=mesh, in_specs=in_specs, out_specs=out_specs, check_vma=False
    )
```

profile of v0, /device:TPU:1, one launch (start us, length us, event | category | flops | bytes accessed | tf_op | source)
XLA Modules:
  0.0 266.6 jit_solution(17880768833656026010)
XLA Ops:
  7.2 2.1 compare_select_fusion
  9.4 0.7 all-gather.5.cloned.1.call-update
  10.1 0.7 compare_select_fusion.1
  11.0 0.7 compare_and_fusion
  11.8 0.7 fusion.18
  12.5 141.4 %all-gather.3.cloned.1.call-done = bf16[32,262144]{1,0:T(8,128)(2,1)} async-done(((bf16[32,8192]{1,0:T(8,128)(2,1)}), bf16[32,262144]{1,0:T(8,128)(2,1)}) %all-gather.3.cloned.1.call-update) | async-done | bytes 16777232 | tf_op jit(solution)/shard_map/all_gather | solution.py:31
  154.0 14.6 %copy_bitcast_fusion = bf16[32,2048,128]{2,0,1:T(8,128)(2,1)} fusion(bf16[32,262144]{1,0:T(8,128)(2,1)} %all-gather.3.cloned.1.call-done), kind=kLoop, calls=%fused_computation.1 | loop fusion | bytes 33554432 | tf_op jit(solution)/shard_map/reshape | solution.py:36
  168.6 12.9 %gather_fusion = bf16[1536,32,128]{2,1,0:T(8,128)(2,1)} fusion(bf16[32,2048,128]{2,0,1:T(8,128)(2,1)} %copy_bitcast_fusion, s32[2048]{0:T(1024)S(1)} %pad_clamp_fusion), kind=kCustom, calls=%fused_computation | custom fusion | bytes 25171968 | tf_op jit(solution)/shard_map/jit(_take)/gather | solution.py:37
  181.5 24.5 %fusion.10 = bf16[64,32,128]{2,1,0:T(8,128)(2,1)S(1)} fusion(bf16[64,24,128,128]{3,2,1,0:T(8,128)(2,1)} %param.11, bf16[64,24,32,128]{3,2,1,0:T(8,128)(2,1)} %bitcast.40, pred[64,24]{1,0:T(8,128)(4,1)S(1)} %copy.30, bf16[64,24]{1,0:T(8,128)(2,1)S(1)} %fusion.18), kind=kOutput, calls=%fused_computation.11 | convolution fusion | flops 1623457792 | bytes 63443456 | tf_op jit(solution)/shard_map/frkc,rkic->fri/dot_general | solution.py:41
  206.1 3.5 %fusion.15 = bf16[256,32]{0,1:T(8,128)(2,1)S(1)} fusion(bf16[256,8192]{1,0:T(8,128)(2,1)} %all-gather.5.cloned.1.call-done, bf16[64,32,128]{2,1,0:T(8,128)(2,1)S(1)} %fusion.10), kind=kOutput, calls=%fused_computation.15 | convolution fusion | flops 134234112 | bytes 4734976 | tf_op jit(solution)/shard_map/dot_general | solution.py:48
  209.6 0.9 broadcast_in_dim.30
  210.5 5.9 %all-to-all-start.1 = ((bf16[32,256,32]{1,2,0:T(8,128)(2,1)}), bf16[32,256,32]{1,2,0:T(8,128)(2,1)S(1)}, u32[]{:S(2)}, u32[]{:S(2)}) async-start(bf16[32,256,32]{1,2,0:T(8,128)(2,1)} %broadcast_in_dim.30), calls=%async_computation.1 | async-start | bytes 1048576 | tf_op jit(solution)/shard_map/all_to_all | solution.py:9
  216.3 0.2 copy.33
  216.6 0.2 convert_element_type.47
  216.8 1.1 copy.34
  217.9 13.9 %all-to-all-done.1 = bf16[32,256,32]{1,2,0:T(8,128)(2,1)S(1)} async-done(((bf16[32,256,32]{1,2,0:T(8,128)(2,1)}), bf16[32,256,32]{1,2,0:T(8,128)(2,1)S(1)}, u32[]{:S(2)}, u32[]{:S(2)}) %all-to-all-start.1) | async-done | bytes 524320 | tf_op jit(solution)/shard_map/all_to_all | solution.py:9
  231.8 7.6 %all-to-all-start = ((bf16[32,8,1024]{2,0,1:T(8,128)(2,1)}), bf16[32,8,1024]{2,0,1:T(8,128)(2,1)S(1)}, u32[]{:S(2)}, u32[]{:S(2)}) async-start(bf16[32,8,1024]{2,0,1:T(8,128)(2,1)} %copy.34), calls=%async_computation | async-start | bytes 1048576 | tf_op jit(solution)/shard_map/all_to_all | solution.py:44
  239.5 9.3 %all-to-all-done = bf16[32,8,1024]{2,0,1:T(8,128)(2,1)S(1)} async-done(((bf16[32,8,1024]{2,0,1:T(8,128)(2,1)}), bf16[32,8,1024]{2,0,1:T(8,128)(2,1)S(1)}, u32[]{:S(2)}, u32[]{:S(2)}) %all-to-all-start) | async-done | bytes 524320 | tf_op jit(solution)/shard_map/all_to_all | solution.py:44
  248.7 0.7 broadcast_in_dim.31
  249.4 4.2 %all-to-all-start.2 = ((bf16[8,256,32]{1,2,0:T(8,128)(2,1)}), bf16[8,256,32]{1,2,0:T(8,128)(2,1)S(1)}, u32[]{:S(2)}, u32[]{:S(2)}) async-start(bf16[8,256,32]{1,2,0:T(8,128)(2,1)} %broadcast_in_dim.31), calls=%async_computation.2 | async-start | bytes 262144 | tf_op jit(solution)/shard_map/all_to_all | solution.py:9
  253.6 0.3 fusion.13
  254.0 1.0 copy.36
  255.0 3.9 %all-to-all-done.2 = bf16[8,256,32]{1,2,0:T(8,128)(2,1)S(1)} async-done(((bf16[8,256,32]{1,2,0:T(8,128)(2,1)}), bf16[8,256,32]{1,2,0:T(8,128)(2,1)S(1)}, u32[]{:S(2)}, u32[]{:S(2)}) %all-to-all-start.2) | async-done | bytes 131104 | tf_op jit(solution)/shard_map/all_to_all | solution.py:9
  258.9 0.8 copy.37
  (12 shorter events, 0.5 us)
Async XLA Ops:
  7.2 246.5 %copy-start = (bf16[256,256]{1,0:T(8,128)(2,1)S(1)}, bf16[256,256]{1,0:T(8,128)(2,1)}, u32[]{:S(2)}) copy-start(bf16[256,256]{1,0:T(8,128)(2,1)} %param.10) | copy-start | bytes 393220
  7.2 146.8 %all-gather.3.cloned.1.call-start = ((), (), s32[]{:S(2)}) async-start(), calls=%async_computation.3 | async-start | bytes 17301504 | tf_op jit(solution)/shard_map/all_gather | solution.py:31
  9.3 196.7 %all-gather.5.cloned.1.call-start = ((), (), s32[]{:S(2)}) async-start(), calls=%async_computation.4 | async-start | bytes 4718592 | tf_op jit(solution)/shard_map/all_gather | solution.py:46
  210.5 21.3 %all-to-all-start.1 = ((bf16[32,256,32]{1,2,0:T(8,128)(2,1)}), bf16[32,256,32]{1,2,0:T(8,128)(2,1)S(1)}, u32[]{:S(2)}, u32[]{:S(2)}) async-start(bf16[32,256,32]{1,2,0:T(8,128)(2,1)} %broadcast_in_dim.30), calls=%async_computation.1 | async-start | bytes 1048576 | tf_op jit(solution)/shard_map/all_to_all | solution.py:9
  231.8 16.9 %all-to-all-start = ((bf16[32,8,1024]{2,0,1:T(8,128)(2,1)}), bf16[32,8,1024]{2,0,1:T(8,128)(2,1)S(1)}, u32[]{:S(2)}, u32[]{:S(2)}) async-start(bf16[32,8,1024]{2,0,1:T(8,128)(2,1)} %copy.34), calls=%async_computation | async-start | bytes 1048576 | tf_op jit(solution)/shard_map/all_to_all | solution.py:44
  249.4 9.5 %all-to-all-start.2 = ((bf16[8,256,32]{1,2,0:T(8,128)(2,1)}), bf16[8,256,32]{1,2,0:T(8,128)(2,1)S(1)}, u32[]{:S(2)}, u32[]{:S(2)}) async-start(bf16[8,256,32]{1,2,0:T(8,128)(2,1)} %broadcast_in_dim.31), calls=%async_computation.2 | async-start | bytes 262144 | tf_op jit(solution)/shard_map/all_to_all | solution.py:9
Sparse Core Ops, SparseCore 0:
  11.2 142.7 all-gather.2
  155.8 32.8 all-gather.4
where the time goes:
time: 267 us
  waiting for transfers between devices  169 us (63%)
  local copies, waits for them, and re-layouts  32.7 us (12%)
  matrix products  28.4 us (11%)
  starting transfers between devices  17.8 us (7%)
  between operations  14.1 us (5%)
  other arithmetic  4.35 us (2%)
    all_gather x1, waiting for transfers between devices, per_device(): whole = lax.all_gather(grad_pre, 'node', axis=1, tiled=True)  141 us
    dot_general x1, matrix products, per_device(): jnp.einsum('frkc,rkic->fri', picked, tiles, preferred_element_type=jnp.fl...  24.5 us
    all_to_all x2, waiting for transfers between devices, sent_to_all(): lax.all_to_all(jnp.broadcast_to(shard[None], (size, *shard.shape)), axis,...  17.8 us
    reshape x1, local copies, waits for them, and re-layouts, per_device(): blocks = whole.reshape(feat_rows, whole.shape[1] // block_size, block_size)  14.6 us
    gather x1, local copies, waits for them, and re-layouts, per_device(): picked = jnp.take(blocks, indices, axis=1)  12.9 us
    all_to_all x2, starting transfers between devices, sent_to_all(): lax.all_to_all(jnp.broadcast_to(shard[None], (size, *shard.shape)), axis,...  10.1 us
    all_to_all x1, waiting for transfers between devices, per_device(): lax.all_to_all(aggregated, 'feat', split_axis=1, concat_axis=0, tiled=True)  9.26 us
    all_to_all x1, starting transfers between devices, per_device(): lax.all_to_all(aggregated, 'feat', split_axis=1, concat_axis=0, tiled=True)  7.57 us
  transfers between devices with their start and end apart: 5, of which 4 were waited for; matrix products, arithmetic and copies ran while one was open for 22% of the time, Pallas kernels for 0%

commit v1 on v0

--- a/solution.py
+++ b/solution.py
@@ -28,7 +28,9 @@
 
 def per_device(out_grad, pre_act, in_act, weight, tiles, indices, counts):
     grad_pre = jnp.where(pre_act > 0, out_grad, jnp.zeros_like(out_grad))
-    whole = lax.all_gather(grad_pre, "node", axis=1, tiled=True)
+    whole = jnp.concatenate(
+        lax.all_to_all(jnp.stack([grad_pre] * lax.axis_size("node")), "node", 0, 0), axis=1
+    )
     feat_rows = whole.shape[0]
     block_size = tiles.shape[2]
     slot_count = tiles.shape[1]

time: 267 us -> 594 us (2.22)
  waiting for transfers between devices: 169 us -> 397 us
  local copies, waits for them, and re-layouts: 32.7 us -> 86.5 us
  starting transfers between devices: 17.8 us -> 64.9 us
    all_to_all x0 -> x1, waiting for transfers between devices: none -> 369 us  [per_device(): lax.all_to_all(jnp.stack([grad_pre] * lax.axis_size('node')), 'node', 0, 0)]
    all_gather x1 -> x0, waiting for transfers between devices: 141 us -> none  [per_device(): whole = lax.all_gather(grad_pre, 'node', axis=1, tiled=True)]
    another operation x0 -> x3, local copies, waits for them, and re-layouts: none -> 50.1 us  [the longest x2 44.1 us: per_device(): blocks = whole.reshape(feat_rows, whole.shape[1] // block_size, block_size)]
    all_to_all x2, starting transfers between devices: 10.1 us -> 44.9 us  [sent_to_all(): lax.all_to_all(jnp.broadcast_to(shard[None], (size, *shard.shape)), axis,...]
    all_to_all x0 -> x1, starting transfers between devices: none -> 12.1 us  [per_device(): lax.all_to_all(jnp.stack([grad_pre] * lax.axis_size('node')), 'node', 0, 0)]
  transfers between devices with their start and end apart: 5 -> 5, of which waited for: 4 -> 4; matrix products, arithmetic and copies ran while one was open for 22% -> 17% of each run, Pallas kernels for 0% -> 0%
where the time goes in v1:
time: 594 us; the launch traced here: 592 us
  waiting for transfers between devices  397 us (67%)
  local copies, waits for them, and re-layouts  86.5 us (15%)
  starting transfers between devices  64.9 us (11%)
  matrix products  28.2 us (5%)
  between operations  14.2 us (2%)
    all_to_all x1, waiting for transfers between devices, per_device(): lax.all_to_all(jnp.stack([grad_pre] * lax.axis_size('node')), 'node', 0, 0)  369 us
    all_to_all x2, starting transfers between devices, sent_to_all(): lax.all_to_all(jnp.broadcast_to(shard[None], (size, *shard.shape)), axis,...  44.9 us
    another operation x2, local copies, waits for them, and re-layouts, per_device(): blocks = whole.reshape(feat_rows, whole.shape[1] // block_size, block_size)  44.1 us
    dot_general x1, matrix products, per_device(): jnp.einsum('frkc,rkic->fri', picked, tiles, preferred_element_type=jnp.fl...  24.3 us
    reshape x1, local copies, waits for them, and re-layouts, per_device(): jnp.concatenate(lax.all_to_all(jnp.stack([grad_pre] * lax.axis_size('node...  18.5 us
    all_to_all x2, waiting for transfers between devices, sent_to_all(): lax.all_to_all(jnp.broadcast_to(shard[None], (size, *shard.shape)), axis,...  17.8 us
    gather x1, local copies, waits for them, and re-layouts, per_device(): picked = jnp.take(blocks, indices, axis=1)  12.7 us
    all_to_all x1, starting transfers between devices, per_device(): lax.all_to_all(jnp.stack([grad_pre] * lax.axis_size('node')), 'node', 0, 0)  12.1 us
  transfers between devices with their start and end apart: 5, of which 4 were waited for; matrix products, arithmetic and copies ran while one was open for 17% of the time, Pallas kernels for 0%

profile of v1, /device:TPU:1, one launch (start us, length us, event | category | flops | bytes accessed | tf_op | source)
XLA Modules:
  0.0 592.1 jit_solution(5452175889187635882)
XLA Ops:
  7.2 1.3 compare_select_fusion
  8.5 5.9 %stack.2 = bf16[32,32,8192]{2,1,0:T(8,128)(2,1)} broadcast(bf16[32,8192]{1,0:T(8,128)(2,1)S(1)} %compare_select_fusion), dimensions={1,2} | broadcast | bytes 17301504 | tf_op jit(solution)/shard_map/stack | solution.py:32
  14.4 12.1 %all-to-all-start = ((bf16[32,32,8192]{2,1,0:T(8,128)(2,1)}), bf16[32,32,8192]{2,1,0:T(8,128)(2,1)}, u32[]{:S(2)}, u32[]{:S(2)}) async-start(bf16[32,32,8192]{2,1,0:T(8,128)(2,1)} %stack.2), calls=%async_computation | async-start | bytes 33554432 | tf_op jit(solution)/shard_map/all_to_all | solution.py:32
  26.6 0.7 all-gather.2.cloned.1.call-update
  27.7 369.1 %all-to-all-done = bf16[32,32,8192]{2,1,0:T(8,128)(2,1)} async-done(((bf16[32,32,8192]{2,1,0:T(8,128)(2,1)}), bf16[32,32,8192]{2,1,0:T(8,128)(2,1)}, u32[]{:S(2)}, u32[]{:S(2)}) %all-to-all-start) | async-done | bytes 16777248 | tf_op jit(solution)/shard_map/all_to_all | solution.py:32
  396.8 18.5 %copy.22 = bf16[32,32,8192]{2,1,0:T(8,128)(2,1)} copy(bf16[32,32,8192]{2,0,1:T(8,128)(2,1)} %bitcast) | data formatting | bytes 33554432 | tf_op jit(solution)/shard_map/reshape | solution.py:31
  415.4 25.6 %reshape_reshape.3 = bf16[32,2048,128]{2,1,0:T(8,128)(2,1)} reshape(bf16[32,32,8192]{2,1,0:T(8,128)(2,1)} %copy.22) | data formatting | bytes 33554432 | tf_op jit(solution)/shard_map/reshape;reshape | solution.py:38
  441.0 18.5 %copy.24 = bf16[32,2048,128]{2,0,1:T(8,128)(2,1)} copy(bf16[32,2048,128]{2,1,0:T(8,128)(2,1)} %reshape_reshape.3) | data formatting | bytes 33554432 | tf_op jit(solution)/shard_map/reshape;reshape | solution.py:38
  459.5 12.7 %gather_fusion = bf16[1536,32,128]{2,1,0:T(8,128)(2,1)} fusion(bf16[32,2048,128]{2,0,1:T(8,128)(2,1)} %copy.24, s32[2048]{0:T(1024)S(1)} %pad_clamp_fusion), kind=kCustom, calls=%fused_computation | custom fusion | bytes 25171968 | tf_op jit(solution)/shard_map/jit(_take)/gather | solution.py:39
  472.2 24.3 %fusion.10 = bf16[64,32,128]{2,1,0:T(8,128)(2,1)S(1)} fusion(bf16[64,24,128,128]{3,2,1,0:T(8,128)(2,1)} %param.11, bf16[64,24,32,128]{3,2,1,0:T(8,128)(2,1)} %bitcast.36, pred[64,24]{1,0:T(8,128)(4,1)S(1)} %copy.21, bf16[64,24]{1,0:T(8,128)(2,1)S(1)} %fusion.18), kind=kOutput, calls=%fused_computation.10 | convolution fusion | flops 1623457792 | bytes 63443456 | tf_op jit(solution)/shard_map/frkc,rkic->fri/dot_general | solution.py:43
  496.5 3.5 fusion.15
  500.1 0.8 broadcast_in_dim.30
  500.9 40.7 %all-to-all-start.2 = ((bf16[32,256,32]{1,2,0:T(8,128)(2,1)}), bf16[32,256,32]{1,2,0:T(8,128)(2,1)S(1)}, u32[]{:S(2)}, u32[]{:S(2)}) async-start(bf16[32,256,32]{1,2,0:T(8,128)(2,1)} %broadcast_in_dim.30), calls=%async_computation.2 | async-start | bytes 1048576 | tf_op jit(solution)/shard_map/all_to_all | solution.py:9
  541.8 0.2 convert_element_type.47
  542.1 1.1 copy.26
  543.1 13.9 %all-to-all-done.2 = bf16[32,256,32]{1,2,0:T(8,128)(2,1)S(1)} async-done(((bf16[32,256,32]{1,2,0:T(8,128)(2,1)}), bf16[32,256,32]{1,2,0:T(8,128)(2,1)S(1)}, u32[]{:S(2)}, u32[]{:S(2)}) %all-to-all-start.2) | async-done | bytes 524320 | tf_op jit(solution)/shard_map/all_to_all | solution.py:9
  557.1 7.8 %all-to-all-start.1 = ((bf16[32,8,1024]{2,0,1:T(8,128)(2,1)}), bf16[32,8,1024]{2,0,1:T(8,128)(2,1)S(1)}, u32[]{:S(2)}, u32[]{:S(2)}) async-start(bf16[32,8,1024]{2,0,1:T(8,128)(2,1)} %copy.26), calls=%async_computation.1 | async-start | bytes 1048576 | tf_op jit(solution)/shard_map/all_to_all | solution.py:46
  565.0 9.3 %all-to-all-done.1 = bf16[32,8,1024]{2,0,1:T(8,128)(2,1)S(1)} async-done(((bf16[32,8,1024]{2,0,1:T(8,128)(2,1)}), bf16[32,8,1024]{2,0,1:T(8,128)(2,1)S(1)}, u32[]{:S(2)}, u32[]{:S(2)}) %all-to-all-start.1) | async-done | bytes 524320 | tf_op jit(solution)/shard_map/all_to_all | solution.py:46
  574.2 0.7 broadcast_in_dim.31
  574.9 4.2 all-to-all-start.3
  579.1 0.4 fusion.13
  579.5 1.0 copy.28
  580.5 3.9 all-to-all-done.3
  584.4 0.8 copy.29
  (18 shorter events, 0.8 us)
Async XLA Ops:
  7.2 572.0 %copy-start = (bf16[256,256]{1,0:T(8,128)(2,1)S(1)}, bf16[256,256]{1,0:T(8,128)(2,1)}, u32[]{:S(2)}) copy-start(bf16[256,256]{1,0:T(8,128)(2,1)} %param.10) | copy-start | bytes 393220
  14.4 12.9 %copy-start.1 = (s32[64,24]{0,1:T(8,128)S(1)}, s32[64,24]{0,1:T(8,128)}, u32[]{:S(2)}) copy-start(s32[64,24]{0,1:T(8,128)} %param.12) | copy-start | bytes 18436
  14.4 13.2 %copy-start.2 = (s32[64]{0:T(128)S(1)}, s32[64]{0:T(128)}, u32[]{:S(2)}) copy-start(s32[64]{0:T(128)} %param.13) | copy-start | bytes 772
  14.4 382.4 %all-to-all-start = ((bf16[32,32,8192]{2,1,0:T(8,128)(2,1)}), bf16[32,32,8192]{2,1,0:T(8,128)(2,1)}, u32[]{:S(2)}, u32[]{:S(2)}) async-start(bf16[32,32,8192]{2,1,0:T(8,128)(2,1)} %stack.2), calls=%async_computation | async-start | bytes 33554432 | tf_op jit(solution)/shard_map/all_to_all | solution.py:32
  26.6 470.0 %all-gather.2.cloned.1.call-start = ((), (), s32[]{:S(2)}) async-start(), calls=%async_computation.4 | async-start | bytes 4718592 | tf_op jit(solution)/shard_map/all_gather | solution.py:48
  500.9 56.1 %all-to-all-start.2 = ((bf16[32,256,32]{1,2,0:T(8,128)(2,1)}), bf16[32,256,32]{1,2,0:T(8,128)(2,1)S(1)}, u32[]{:S(2)}, u32[]{:S(2)}) async-start(bf16[32,256,32]{1,2,0:T(8,128)(2,1)} %broadcast_in_dim.30), calls=%async_computation.2 | async-start | bytes 1048576 | tf_op jit(solution)/shard_map/all_to_all | solution.py:9
  557.1 17.2 %all-to-all-start.1 = ((bf16[32,8,1024]{2,0,1:T(8,128)(2,1)}), bf16[32,8,1024]{2,0,1:T(8,128)(2,1)S(1)}, u32[]{:S(2)}, u32[]{:S(2)}) async-start(bf16[32,8,1024]{2,0,1:T(8,128)(2,1)} %copy.26), calls=%async_computation.1 | async-start | bytes 1048576 | tf_op jit(solution)/shard_map/all_to_all | solution.py:46
  574.9 9.5 %all-to-all-start.3 = ((bf16[8,256,32]{1,2,0:T(8,128)(2,1)}), bf16[8,256,32]{1,2,0:T(8,128)(2,1)S(1)}, u32[]{:S(2)}, u32[]{:S(2)}) async-start(bf16[8,256,32]{1,2,0:T(8,128)(2,1)} %broadcast_in_dim.31), calls=%async_computation.3 | async-start | bytes 262144 | tf_op jit(solution)/shard_map/all_to_all | solution.py:9
Sparse Core Ops, SparseCore 0:
  29.2 36.6 all-gather.1
